TPU v7x, 32 devices: a whole 2x2x4 slice. The times are simulated.
32 devices in a mesh: feat: 16 (over z, x, core), samp: 2 (over y).
Axes of the slice: x: 2, y: 2, z: 4, core: 2. Of those that a mesh axis runs over, the one named last changes fastest.
Arguments:
- features: bfloat16 [4096, 16384], P('samp', 'feat'), may hold values from -0.046875 to 0.046875
- labels: int32 [4096], P('samp'), may hold values 0 or 1
- weights: float32 [16384], P('feat'), may hold values from -6 to 6
- sampled: int32 [2048], P('samp'), may hold values from 0 to 2047
Outputs:
- step: float32 [16384], P('feat')
Inputs may be any that keep to these rules, and one draw needn't show every extreme that they name: `sampled`: entries i * 1024 to (i + 1) * 1024 - 1 name rows of the i-th block of 2048 data rows, counted from that block's start; rows may repeat.
All inputs are finite; a program needn't handle non-finite values. No bound on the sum of `labels` on one device may be relied on, other than what follows from the above.
Results may differ from a plain program's by a relative error of at most 0.0025.
Values may be sent and summed in bfloat16 or wider, within the bound.
A program may use at most 64 MiB of HBM per device.

v0:
```python
import jax
import jax.numpy as jnp
from jax import lax
from jax.sharding import PartitionSpec as P

F = 16384
BLK = 512
ITERS = 3


RIDGE_COEF = 0.05


def partner_2(value, axis, apart):
    mask = 2**apart
    pairs = [(source, source ^ mask) for source in range(lax.axis_size(axis))]
    return lax.ppermute(value, axis, pairs)


def split_parts(vector):
    upper_part = vector.astype(jnp.bfloat16)
    widened = lax.optimization_barrier(upper_part).astype(jnp.float32)
    lower_part = (vector - widened).astype(jnp.bfloat16)
    return (upper_part, lower_part)


def matrix_vector(matrix, vector):
    upper_part, lower_part = split_parts(vector)
    return jnp.dot(matrix, upper_part, preferred_element_type=jnp.float32) + jnp.dot(
        matrix, lower_part, preferred_element_type=jnp.float32
    )


def vector_matrix(vector, matrix):
    upper_part, lower_part = split_parts(vector)
    return jnp.dot(upper_part, matrix, preferred_element_type=jnp.float32) + jnp.dot(
        lower_part, matrix, preferred_element_type=jnp.float32
    )


def block_solve(factors, rhs_blocks):
    forward = jax.vmap(
        lambda factor, column: jax.scipy.linalg.solve_triangular(factor, column, lower=True)
    )(factors, rhs_blocks)
    return jax.vmap(
        lambda factor, column: jax.scipy.linalg.solve_triangular(
            factor, column, lower=True, trans=1
        )
    )(factors, forward)


def local_blocks(scaled):
    blocks = scaled.reshape(scaled.shape[0], scaled.shape[1] // BLK, BLK)
    return jnp.einsum("hkb,hkc->kbc", blocks, blocks, preferred_element_type=jnp.float32)


def per_device(features, labels, weights, sampled):
    columns = features.shape[1]
    sample_rows = sampled.shape[0]
    groups = lax.axis_size("samp")
    row_total = features.shape[0] * groups
    hess_total = sample_rows * groups
    ridge_term = RIDGE_COEF / F
    paired = columns < BLK
    upper_side = lax.axis_index("feat") % 2 == 1
    margin = lax.psum(matrix_vector(features, weights), "feat")
    probability = jax.nn.sigmoid(margin)
    residue = probability - labels.astype(jnp.float32)
    gradient = lax.psum(vector_matrix(residue, features), "samp") / row_total + ridge_term * weights
    chosen = jnp.take(probability, sampled)
    root_curv = jnp.sqrt(chosen * (1.0 - chosen))
    scaled = (jnp.take(features, sampled, axis=0) * root_curv[:, None]).astype(jnp.bfloat16)
    if paired:
        partner = partner_2(scaled, "feat", 0)
        joined = jnp.where(
            upper_side, jnp.concatenate([partner, scaled], 1), jnp.concatenate([scaled, partner], 1)
        )
        partial_gram = jnp.einsum("hb,hc->bc", joined, joined, preferred_element_type=jnp.float32)[
            None
        ]
    else:
        partial_gram = local_blocks(scaled)
    summed = lax.psum(partial_gram, "samp")
    gram = summed / hess_total + ridge_term * jnp.eye(BLK, dtype=jnp.float32)
    factors = jnp.linalg.cholesky(gram)

    def precondition(vector):
        if paired:
            other = partner_2(vector, "feat", 0)
            joined_vec = jnp.where(
                upper_side, jnp.concatenate([other, vector]), jnp.concatenate([vector, other])
            )[None]
            solved = block_solve(factors, joined_vec)[0]
            return jnp.where(upper_side, solved[columns:], solved[:columns])
        return block_solve(factors, vector.reshape(-1, BLK)).reshape(columns)

    def curvature(vector):
        image_rows = lax.psum(matrix_vector(scaled, vector), "feat")
        back = lax.psum(vector_matrix(image_rows, scaled), "samp")
        return back / hess_total + ridge_term * vector

    solution = jnp.zeros((columns,), jnp.float32)
    residual = -gradient

    def both_dots(resid_vec, precond_vec, image_vec):
        return lax.psum(
            (jnp.sum(resid_vec * precond_vec), jnp.sum(image_vec * precond_vec)), "feat"
        )

    precond = precondition(residual)
    image = curvature(precond)
    rz_now, wz_now = both_dots(residual, precond, image)
    alpha = rz_now / wz_now
    direction = precond
    along = image
    for iteration in range(ITERS):
        solution = solution + alpha * direction
        residual = residual - alpha * along
        if iteration + 1 < ITERS:
            precond = precondition(residual)
            image = curvature(precond)
            fresh, wz_now = both_dots(residual, precond, image)
            beta = fresh / rz_now
            alpha = fresh / (wz_now - beta * fresh / alpha)
            direction = precond + beta * direction
            along = image + beta * along
            rz_now = fresh
    return solution


def solution(mesh):
    placed = (P("samp", "feat"), P("samp"), P("feat"), P("samp"))
    return jax.shard_map(
        per_device, mesh=mesh, in_specs=placed, out_specs=P("feat"), check_vma=False
    )
```

profile of v0, /device:TPU:0, one launch (start us, length us, event | category | flops | bytes accessed | tf_op | source)
XLA Modules:
  0.0 659.0 jit_solution(305277117507867407)
XLA Ops:
  7.9 3.5 fusion.99
  12.7 35.4 %psum.105 = f32[2048]{0:T(1024)S(1)} all-reduce(f32[2048]{0:T(1024)S(1)} %add.146), channel_id=1, replica_groups=mesh['feat'=16,'samp'=2] {'feat'}, use_global_device_ids=true, to_apply=%region_0.0 | all-reduce | flops 2048 | bytes 16384 | tf_op jit(solution)/shard_map/psum | solution.py:66
  48.2 7.7 %gather_fusion = bf16[1024,1024]{1,0:T(8,128)(2,1)S(1)} fusion(bf16[2048,1024]{1,0:T(8,128)(2,1)} %param.8, s32[1024]{0:T(1024)S(1)} %fusion.77), kind=kCustom, calls=%fused_computation | custom fusion | bytes 4198400 | tf_op jit(solution)/shard_map/jit(_take)/gather | solution.py:72
  55.9 6.2 gather_fusion.1
  64.7 4.8 fusion
  69.6 3.0 fusion.101
  74.3 5.1 psum.106
  83.0 47.0 %all-reduce.6.cloned.1.call-done = f32[2,512,512]{1,2,0:T(8,128)} async-done(((f32[2,512,512]{1,2,0:T(8,128)}), f32[2,512,512]{1,2,0:T(8,128)}) %all-reduce.6.cloned.1.call-update) | async-done | bytes 2097168 | tf_op jit(solution)/shard_map/psum | solution.py:83
  130.0 3.6 multiply_add_fusion
  133.5 3.3 copy.40
  136.8 3.2 fusion.1
  141.4 23.5 %custom-call.37 = f32[2,128,128]{2,1,0:T(8,128)S(1)} custom-call(f32[2,128,128]{2,1,0:T(8,128)S(1)} %cholesky.274), custom_call_target="Cholesky" | custom-call | tf_op jit(solution)/shard_map/jit(cholesky)/cholesky | solution.py:85
  164.9 19.7 %custom-call.38 = f32[2,1,128,128]{2,3,1,0:T(8,128)S(1)} custom-call(f32[2,1,128,128]{3,2,1,0:T(8,128)S(1)} %select_bitcast_fusion.2), custom_call_target="InvertDiagBlocksLowerTriangular" | custom-call | tf_op jit(solution)/shard_map/jit(cholesky)/cholesky | solution.py:85
  189.9 23.5 %custom-call.39 = f32[2,128,128]{2,1,0:T(8,128)S(1)} custom-call(f32[2,128,128]{2,1,0:T(8,128)S(1)} %cholesky.278), custom_call_target="Cholesky" | custom-call | tf_op jit(solution)/shard_map/jit(cholesky)/cholesky | solution.py:85
  214.1 19.8 %custom-call.40 = f32[2,1,128,128]{2,3,1,0:T(8,128)S(1)} custom-call(f32[2,1,128,128]{3,2,1,0:T(8,128)S(1)} %get-tuple-element.84), custom_call_target="InvertDiagBlocksLowerTriangular" | custom-call | tf_op jit(solution)/shard_map/jit(cholesky)/cholesky | solution.py:85
  236.8 23.5 %custom-call.41 = f32[2,128,128]{2,1,0:T(8,128)S(1)} custom-call(f32[2,128,128]{2,1,0:T(8,128)S(1)} %cholesky.283), custom_call_target="Cholesky" | custom-call | tf_op jit(solution)/shard_map/jit(cholesky)/cholesky | solution.py:85
  261.0 19.7 %custom-call.42 = f32[2,1,128,128]{2,3,1,0:T(8,128)S(1)} custom-call(f32[2,1,128,128]{3,2,1,0:T(8,128)S(1)} %get-tuple-element.82), custom_call_target="InvertDiagBlocksLowerTriangular" | custom-call | tf_op jit(solution)/shard_map/jit(cholesky)/cholesky | solution.py:85
  283.4 23.7 %custom-call.43 = f32[2,128,128]{2,1,0:T(8,128)S(1)} custom-call(f32[2,128,128]{2,1,0:T(8,128)S(1)} %convolution_subtract_fusion.2), custom_call_target="Cholesky" | custom-call | tf_op jit(solution)/shard_map/jit(cholesky)/cholesky | solution.py:85
  308.1 3.4 select_select_fusion
  311.5 14.2 %while.12 = (s32[]{:T(128)}, f32[2,512,512]{2,1,0:T(8,128)}, s32[4,2]{0,1:T(2,128)S(1)}, f32[4,2,128,128]{3,2,0,1:T(8,128)}, s32[]{:T(128)}) while((s32[]{:T(128)}, f32[2,512,512]{2,1,0:T(8,128)}, s32[4,2]{0,1:T(2,128)S(1)}, f32[4,2,128,128]{3,2,0,1:T(8,128)}, s32[]{:T(128)}) %tuple.52), condition=%wide.while_cond.1, body=%wide.while_body.1.sunk | while | flops 2 | bytes 263777 | solution.py:46
  315.6 3.0 bitcast_dynamic-update-slice_fusion.2
  319.2 3.0 bitcast_dynamic-update-slice_fusion.2
  325.7 79.4 %custom-call.49 = f32[2,4,128,128]{2,3,1,0:T(8,128)S(1)} custom-call(f32[2,4,128,128]{3,2,1,0:T(8,128)} %bitcast.542), custom_call_target="InvertDiagBlocksLowerTriangular" | custom-call | tf_op jit(solution)/shard_map/vmap(jit(_solve_triangular))/triangular_solve | solution.py:46
  416.6 33.0 %psum.109 = f32[1024]{0:T(1024)S(1)} all-reduce(f32[1024]{0:T(1024)S(1)} %add.155), channel_id=1, replica_groups=mesh['feat'=16,'samp'=2] {'feat'}, use_global_device_ids=true, to_apply=%region_13.16 | all-reduce | flops 1024 | bytes 8192 | tf_op jit(solution)/shard_map/psum | solution.py:98
  450.4 4.9 psum.110
  455.9 30.4 %all-reduce.3 = (f32[]{:T(128)}, f32[]{:T(128)}) all-reduce(f32[]{:T(128)} %get-tuple-element.62, f32[]{:T(128)} %get-tuple-element.61), channel_id=1, replica_groups=mesh['feat'=16,'samp'=2] {'feat'}, use_global_device_ids=true, to_apply=%region_12.15 | all-reduce | flops 2 | bytes 16 | tf_op jit(solution)/shard_map/psum | solution.py:106
  499.1 29.5 %psum.113 = f32[1024]{0:T(1024)S(1)} all-reduce(f32[1024]{0:T(1024)S(1)} %add.158), channel_id=1, replica_groups=mesh['feat'=16,'samp'=2] {'feat'}, use_global_device_ids=true, to_apply=%region_19.22 | all-reduce | flops 1024 | bytes 8192 | tf_op jit(solution)/shard_map/psum | solution.py:98
  529.4 4.9 psum.114
  535.0 30.1 %all-reduce.2 = (f32[]{:T(128)}, f32[]{:T(128)}) all-reduce(f32[]{:T(128)} %get-tuple-element.60, f32[]{:T(128)} %get-tuple-element.59), channel_id=1, replica_groups=mesh['feat'=16,'samp'=2] {'feat'}, use_global_device_ids=true, to_apply=%region_18.21 | all-reduce | flops 2 | bytes 16 | tf_op jit(solution)/shard_map/psum | solution.py:106
  581.0 29.5 %psum.117 = f32[1024]{0:T(1024)S(1)} all-reduce(f32[1024]{0:T(1024)S(1)} %add.164), channel_id=1, replica_groups=mesh['feat'=16,'samp'=2] {'feat'}, use_global_device_ids=true, to_apply=%region_25.28 | all-reduce | flops 1024 | bytes 8192 | tf_op jit(solution)/shard_map/psum | solution.py:98
  611.4 4.9 psum.118
  616.9 30.2 %all-reduce.1 = (f32[]{:T(128)}, f32[]{:T(128)}) all-reduce(f32[]{:T(128)} %get-tuple-element.58, f32[]{:T(128)} %get-tuple-element.57), channel_id=1, replica_groups=mesh['feat'=16,'samp'=2] {'feat'}, use_global_device_ids=true, to_apply=%region_24.27 | all-reduce | flops 2 | bytes 16 | tf_op jit(solution)/shard_map/psum | solution.py:106
  (204 shorter events, 72.7 us)
Async XLA Ops:
  6.5 123.4 %all-reduce.6.cloned.1.call-start = ((), (), s32[]{:S(2)}) async-start(), calls=%async_computation | async-start | bytes 4194304 | tf_op jit(solution)/shard_map/psum | solution.py:83
  7.9 3.5 copy-start
  11.5 36.7 %copy-start.5 = (s32[2048]{0:T(1024)S(1)}, s32[2048]{0:T(1024)}, u32[]{:S(2)}) copy-start(s32[2048]{0:T(1024)} %param.9) | copy-start | bytes 24580
  11.5 36.7 %copy-start.8 = (s32[1024]{0:T(1024)S(1)}, s32[1024]{0:T(1024)}, u32[]{:S(2)}) copy-start(s32[1024]{0:T(1024)} %param.11) | copy-start | bytes 12292
  55.9 6.2 copy-start.2
  69.6 4.1 copy-start.1
  73.7 5.8 copy-start.4
  79.5 3.5 copy-start.6
  140.0 1.4 copy-start.3
  308.1 97.0 %slice-start = ((f32[2,512,1]{1,0,2:T(2,128)}), f32[2,128,1]{1,0,2:T(2,128)S(1)}, s32[]{:S(2)}) async-start(f32[2,512,1]{1,0,2:T(2,128)} %copy-done.6), calls=%async_computation.1 | async-start | bytes 2048 | tf_op jit(solution)/shard_map/vmap(jit(_solve_triangular))/triangular_solve | solution.py:43
  308.1 98.5 %copy-start.7 = (f32[2,512,1]{1,0,2:T(2,128)S(1)}, f32[2,512,1]{1,0,2:T(2,128)}, u32[]{:S(2)}) copy-start(f32[2,512,1]{1,0,2:T(2,128)} %copy-done.6) | copy-start | bytes 12292
Sparse Core Ops, SparseCore 0:
  69.7 60.2 all-reduce.5
where the time goes:
time: 666 us; the launch traced here: 659 us
  other arithmetic  253 us (38%)
  blocking collectives  238 us (36%)
  matrix products  58.7 us (9%)
  waiting for transfers between devices  47 us (7%)
  local copies, waits for them, and re-layouts  38.2 us (6%)
  between operations  24.2 us (4%)
    another operation x16, other arithmetic, per_device(): factors = jnp.linalg.cholesky(gram)  156 us
    psum x3, blocking collectives, curvature(): image_rows = lax.psum(matrix_vector(scaled, vector), 'feat')  92 us
    psum x3, blocking collectives, both_dots(): lax.psum((jnp.sum(resid_vec * precond_vec), jnp.sum(image_vec * precond_v...  90.7 us
    another operation x20, other arithmetic, block_solve(): jax.scipy.linalg.solve_triangular(factor, column, lower=True, trans=1)  83 us
    psum x1, waiting for transfers between devices, per_device(): summed = lax.psum(partial_gram, 'samp')  47 us
    psum x1, blocking collectives, per_device(): margin = lax.psum(matrix_vector(features, weights), 'feat')  35.4 us
    another operation x21, matrix products, block_solve(): jax.scipy.linalg.solve_triangular(factor, column, lower=True, trans=1)  15 us
    another operation x21, matrix products, block_solve(): jax.scipy.linalg.solve_triangular(factor, column, lower=True)  15 us
  transfers between devices with their start and end apart: 1, of which 1 were waited for; matrix products, arithmetic and copies ran while one was open for 1% of the time, Pallas kernels for 0%

commit v1 on v0

--- a/solution.py
+++ b/solution.py
@@ -1,11 +1,17 @@
+import functools
+
 import jax
 import jax.numpy as jnp
 from jax import lax
+from jax.experimental import pallas as pl
+from jax.experimental.pallas import tpu as pltpu
 from jax.sharding import PartitionSpec as P
 
 F = 16384
 BLK = 512
 ITERS = 3
+QUAD = 4
+MESH = pl.DeviceIdType.MESH
 
 
 RIDGE_COEF = 0.05
@@ -127,9 +133,447 @@
             rz_now = fresh
     return solution
 
+def split_rows(row):
+    top = row.astype(jnp.bfloat16).astype(jnp.float32)
+    rest = row - top
+    middle = rest.astype(jnp.bfloat16).astype(jnp.float32)
+    bottom = rest - middle
+    shape = (16, row.shape[1])
+    line = lax.broadcasted_iota(jnp.int32, shape, 0)
+    spread = lambda part: jnp.broadcast_to(part, shape)
+    picked = jnp.where(
+        line == 0,
+        spread(top),
+        jnp.where(line == 1, spread(middle), jnp.where(line == 2, spread(bottom), 0.0)),
+    )
+    return picked.astype(jnp.bfloat16)
+
+
+def add_rows(parts):
+    return parts[0:1] + parts[1:2] + parts[2:3]
+
+
+def mxu(left, right, left_dim, right_dim):
+    return lax.dot_general(
+        left, right, (((left_dim,), (right_dim,)), ((), ())), preferred_element_type=jnp.float32
+    )
+
+
+def row_times(row, matrix):
+    return add_rows(mxu(split_rows(row), matrix, 1, 0))
+
+
+def row_times_transposed(row, matrix):
+    return add_rows(mxu(split_rows(row), matrix, 1, 1))
+
+
+def place():
+    feat = lax.axis_index("feat")
+    samp = lax.axis_index("samp")
+    return feat // QUAD, feat % QUAD, samp
+
+
+def greet(peers):
+    barrier = pltpu.get_barrier_semaphore()
+    for peer in peers:
+        pl.semaphore_signal(barrier, inc=1, device_id=peer, device_id_type=MESH)
+    return lambda: pl.semaphore_wait(barrier, len(peers))
+
+
+def remote(source, target, send_sem, recv_sem, peer):
+    return pltpu.make_async_remote_copy(
+        src_ref=source,
+        dst_ref=target,
+        send_sem=send_sem,
+        recv_sem=recv_sem,
+        device_id=peer,
+        device_id_type=MESH,
+    )
+
+
+def start_exchange(slots, mine, peers, send_sems, recv_sems):
+    copies = []
+    for number, peer in enumerate(peers):
+        copy = remote(
+            slots.at[mine], slots.at[mine], send_sems.at[number], recv_sems.at[number], peer
+        )
+        copy.start()
+        copies.append(copy)
+    return copies
+
+
+def finish(copies):
+    for copy in copies:
+        copy.wait()
+
+
+def total_of(slots, count):
+    value = slots[0]
+    for number in range(1, count):
+        value = value + slots[number]
+    return value
+
+
+def quad_peers(depth, quarter, samp):
+    return [{"feat": depth * QUAD + (quarter + k) % QUAD, "samp": samp} for k in range(1, QUAD)]
+
+
+def depth_peers(layers, depth, quarter, samp):
+    return [
+        {"feat": ((depth + k) % layers) * QUAD + quarter, "samp": samp} for k in range(1, layers)
+    ]
+
+
+def plane_peers(depth, quarter, samp):
+    member = samp * QUAD + quarter
+    peers = []
+    for k in range(1, 2 * QUAD):
+        other = (member + k) % (2 * QUAD)
+        peers.append({"feat": depth * QUAD + other % QUAD, "samp": other // QUAD})
+    return peers
+
+
+CHUNKS = 4
+
+
+def gram_kernel(
+    layers, features, weights, labels, sampled,
+    scaled, gram, gradient,
+    chosen, own_rows, sent_rows, came_rows, quad_slots, depth_slots, root_sent, root_came, grad_sent, grad_came,
+    ship_send, ship_recv, quad_send, quad_recv, depth_send, depth_recv, small_send, small_recv,
+):
+    depth, quarter, samp = place()
+    rows, columns = features.shape
+    samples = sampled.shape[0]
+    half = columns // 2
+    partner = {"feat": depth * QUAD + quarter, "samp": 1 - samp}
+    across = quad_peers(depth, quarter, samp)
+    along = depth_peers(layers, depth, quarter, samp)
+    wait_all = greet([partner] + across + along)
+    mine_at = pl.multiple_of(samp * half, 128)
+    other_at = pl.multiple_of((1 - samp) * half, 128)
+    piece = samples // CHUNKS
+
+    quad_slots[quarter] = row_times_transposed(weights[...], features[...])
+    wait_all()
+    quad_copies = start_exchange(quad_slots, quarter, across, quad_send, quad_recv)
+
+    def ship(number):
+        first = number * piece
+        return remote(
+            sent_rows.at[pl.ds(first, piece)],
+            came_rows.at[pl.ds(first, piece)],
+            ship_send.at[number],
+            ship_recv.at[number],
+            partner,
+        )
+
+    def pick(number, carry):
+        first = pl.multiple_of(number * piece, 128)
+        names = jnp.broadcast_to(sampled[pl.ds(first, piece), :], (piece, rows))
+        hot = jnp.where(lax.broadcasted_iota(jnp.int32, (piece, rows), 1) == names, 1.0, 0.0)
+        hot = hot.astype(jnp.bfloat16)
+        chosen[pl.ds(first, piece), :] = hot
+        sent_rows[pl.ds(first, piece), :] = mxu(hot, features[:, pl.ds(other_at, half)], 1, 0).astype(
+            jnp.bfloat16
+        )
+        ship(number).start()
+        return carry
+
+    lax.fori_loop(0, CHUNKS, pick, 0)
+    finish(quad_copies)
+    depth_slots[depth] = total_of(quad_slots, QUAD)
+    depth_copies = start_exchange(depth_slots, depth, along, depth_send, depth_recv)
+
+    def pick_own(number, carry):
+        first = pl.multiple_of(number * piece, 128)
+        own_rows[pl.ds(first, piece), :] = mxu(
+            chosen[pl.ds(first, piece), :], features[:, pl.ds(mine_at, half)], 1, 0
+        ).astype(jnp.bfloat16)
+        return carry
+
+    lax.fori_loop(0, CHUNKS, pick_own, 0)
+    finish(depth_copies)
+    margin = total_of(depth_slots, layers)
+    probability = 1.0 / (1.0 + jnp.exp(-margin))
+    root = jnp.sqrt(probability * (1.0 - probability))
+    own_root = row_times_transposed(root, chosen[...])
+    root_sent[...] = own_root
+    root_copy = remote(root_sent, root_came, small_send.at[0], small_recv.at[0], partner)
+    root_copy.start()
+    residue = probability - labels[...].astype(jnp.float32)
+    grad_sent[...] = row_times(residue, features[:, pl.ds(other_at, half)])
+    grad_copy = remote(grad_sent, grad_came, small_send.at[1], small_recv.at[1], partner)
+    grad_copy.start()
+    own_grad = row_times(residue, features[:, pl.ds(mine_at, half)])
+
+    def scale_into(source, root_row, start):
+        factor = jnp.transpose(jnp.broadcast_to(root_row, (128, samples)))
+        for column in range(0, half, 128):
+            wide = source[:, column : column + 128].astype(jnp.float32) * factor
+            scaled[pl.ds(start, samples), column : column + 128] = wide.astype(jnp.bfloat16)
+
+    mine_row = pl.multiple_of(samp * samples, 128)
+    other_row = pl.multiple_of((1 - samp) * samples, 128)
+    scale_into(own_rows, own_root, mine_row)
+    own_block = scaled[pl.ds(mine_row, samples), :]
+    gram[...] = mxu(own_block, own_block, 0, 0)
+
+    def settle(number, carry):
+        ship(number).wait()
+        return carry
+
+    root_copy.wait()
+    grad_copy.wait()
+    ridge_term = RIDGE_COEF / F
+    gradient[...] = (own_grad + grad_came[...]) / (2 * rows) + ridge_term * weights[
+        :, pl.ds(mine_at, half)
+    ]
+    lax.fori_loop(0, CHUNKS, settle, 0)
+    scale_into(came_rows, root_came[...], other_row)
+    other_block = scaled[pl.ds(other_row, samples), :]
+    both = gram[...] + mxu(other_block, other_block, 0, 0)
+    diagonal = lax.broadcasted_iota(jnp.int32, both.shape, 0) == lax.broadcasted_iota(
+        jnp.int32, both.shape, 1
+    )
+    gram[...] = both / (2 * samples) + jnp.where(diagonal, ridge_term, 0.0)
+
+
+SQUARINGS = 8
+POLISH = 2
+LIMIT = 60
+
+
+def halves(value):
+    top = value.astype(jnp.bfloat16)
+    return top, (value - top.astype(jnp.float32)).astype(jnp.bfloat16)
+
+
+def inverse_kernel(gram, upper, lower, unit, inverse):
+    order = gram.shape[0]
+    bound = jnp.max(jnp.sum(jnp.abs(gram[...]), axis=0, keepdims=True))
+    shape = (order, order)
+    eye = jnp.where(
+        lax.broadcasted_iota(jnp.int32, shape, 0) == lax.broadcasted_iota(jnp.int32, shape, 1),
+        1.0,
+        0.0,
+    )
+    normed = gram[...] / bound
+    unit[...] = normed
+    power = eye - normed
+    inverse[...] = eye + power
+
+    def square(_, power_now):
+        squared = mxu(power_now, power_now, 1, 0)
+        power_next = squared.astype(jnp.bfloat16)
+        value = inverse[...]
+        inverse[...] = value + mxu(value.astype(jnp.bfloat16), power_next, 1, 0)
+        return power_next
+
+    lax.fori_loop(0, SQUARINGS, square, power.astype(jnp.bfloat16))
+    unit_top, unit_low = halves(unit[...])
+
+    def polish(_, size):
+        value = inverse[...]
+        top, low = halves(value)
+        product = mxu(unit_top, top, 1, 0) + mxu(unit_top, low, 1, 0) + mxu(unit_low, top, 1, 0)
+        left = eye - product
+        inverse[...] = value + mxu(top, left.astype(jnp.bfloat16), 1, 0)
+        return jnp.sum(left * left)
+
+    size = lax.fori_loop(0, POLISH, polish, jnp.float32(0.0))
+    settled = size < 0.0025
+
+    @pl.when(jnp.logical_not(settled))
+    def _():
+        inverse[...] = eye
+
+        def exact(left, right):
+            return jnp.dot(
+                left, right, precision=lax.Precision.HIGHEST, preferred_element_type=jnp.float32
+            )
+
+        def going(state):
+            count, size_now = state
+            return jnp.logical_and(count < LIMIT, size_now > 1e-8)
+
+        def step(state):
+            count, _ = state
+            value = inverse[...]
+            left = eye - exact(unit[...], value)
+            fresh = value + exact(value, left)
+            inverse[...] = 0.5 * (fresh + jnp.transpose(fresh))
+            return count + 1, jnp.sum(left * left)
+
+        lax.while_loop(going, step, (jnp.int32(0), jnp.float32(1.0)))
+
+    top, low = halves(inverse[...] / bound)
+    upper[...] = top
+    lower[...] = low
+
+
+def descent_kernel(
+    layers, scaled, upper, lower, gradient,
+    step,
+    plane_slots, depth_slots, last_sent, last_came,
+    plane_send, plane_recv, depth_send, depth_recv, last_send, last_recv,
+):
+    depth, quarter, samp = place()
+    samples, half = scaled.shape
+    partner = {"feat": depth * QUAD + quarter, "samp": 1 - samp}
+    plane = plane_peers(depth, quarter, samp)
+    along = depth_peers(layers, depth, quarter, samp)
+    wait_all = greet(plane + along)
+    member = samp * QUAD + quarter
+    ridge_term = RIDGE_COEF / F
+    lane = lax.broadcasted_iota(jnp.int32, (1, 128), 1)
+
+    def precondition(vector):
+        parts = split_rows(vector)
+        return add_rows(mxu(parts, upper[...], 1, 0) + mxu(parts, lower[...], 1, 0))
+
+    def total(row):
+        return jnp.sum(row, axis=1, keepdims=True)
+
+    residual = -gradient[...]
+    answer = jnp.zeros_like(residual)
+    direction = jnp.zeros_like(residual)
+    along_rows = None
+    rz_now = None
+    length = None
+    for iteration in range(ITERS):
+        precond = precondition(residual)
+        numbers = jnp.where(
+            lane == 0,
+            total(residual * precond),
+            jnp.where(
+                lane == 1,
+                total(precond * precond),
+                jnp.where(lane == 2, total(precond * direction), 0.0),
+            ),
+        )
+        mine = plane_slots.at[iteration, member]
+        mine[:, :samples] = row_times_transposed(precond, scaled[...])
+        mine[:, samples:] = numbers
+        if iteration == 0:
+            wait_all()
+        finish(
+            start_exchange(
+                plane_slots.at[iteration], member, plane, plane_send.at[iteration], plane_recv.at[iteration]
+            )
+        )
+        depth_slots[iteration, depth] = total_of(plane_slots.at[iteration], 2 * QUAD)
+        finish(
+            start_exchange(
+                depth_slots.at[iteration], depth, along, depth_send.at[iteration], depth_recv.at[iteration]
+            )
+        )
+        summed = total_of(depth_slots.at[iteration], layers)
+        image_rows = summed[:, :samples]
+        fresh = summed[:, samples : samples + 1]
+        square = summed[:, samples + 1 : samples + 2]
+        cross = summed[:, samples + 2 : samples + 3]
+        if iteration == 0:
+            direction = precond
+            along_rows = image_rows
+            length = square
+        else:
+            beta = fresh / rz_now
+            direction = precond + beta * direction
+            along_rows = image_rows + beta * along_rows
+            length = square + 2.0 * beta * cross + beta * beta * length
+        rz_now = fresh
+        alpha = rz_now / (total(along_rows * along_rows) / samples + ridge_term * length)
+        answer = answer + alpha * direction
+        if iteration + 1 < ITERS:
+            image = row_times(along_rows, scaled[...]) / samples + ridge_term * direction
+            residual = residual - alpha * image
+    last_sent[...] = answer
+    final = remote(last_sent, last_came, last_send.at[0], last_recv.at[0], partner)
+    final.start()
+    step[:, pl.ds(pl.multiple_of(samp * half, 128), half)] = answer
+    final.wait()
+    step[:, pl.ds(pl.multiple_of((1 - samp) * half, 128), half)] = last_came[...]
+
+
+def split_device(features, labels, weights, sampled):
+    rows, columns = features.shape
+    samples = sampled.shape[0]
+    half = columns // 2
+    layers = lax.axis_size("feat") // QUAD
+    shaped = jax.ShapeDtypeStruct
+    whole = pl.BlockSpec(memory_space=pltpu.VMEM)
+    dma = pltpu.SemaphoreType.DMA
+    vmem = pltpu.VMEM
+    scaled, gram, gradient = pl.pallas_call(
+        functools.partial(gram_kernel, layers),
+        out_shape=(
+            shaped((2 * samples, half), jnp.bfloat16),
+            shaped((half, half), jnp.float32),
+            shaped((1, half), jnp.float32),
+        ),
+        in_specs=[whole] * 4,
+        out_specs=(whole,) * 3,
+        scratch_shapes=[
+            vmem((samples, rows), jnp.bfloat16),
+            vmem((samples, half), jnp.bfloat16),
+            vmem((samples, half), jnp.bfloat16),
+            vmem((samples, half), jnp.bfloat16),
+            vmem((QUAD, 1, rows), jnp.float32),
+            vmem((layers, 1, rows), jnp.float32),
+            vmem((1, samples), jnp.float32),
+            vmem((1, samples), jnp.float32),
+            vmem((1, half), jnp.float32),
+            vmem((1, half), jnp.float32),
+            dma((CHUNKS,)),
+            dma((CHUNKS,)),
+            dma((QUAD - 1,)),
+            dma((QUAD - 1,)),
+            dma((layers - 1,)),
+            dma((layers - 1,)),
+            dma((2,)),
+            dma((2,)),
+        ],
+        compiler_params=pltpu.CompilerParams(collective_id=0, has_side_effects=True),
+    )(features, weights[None, :], labels[None, :], sampled[:, None])
+    upper, lower = pl.pallas_call(
+        inverse_kernel,
+        out_shape=(shaped((half, half), jnp.bfloat16),) * 2,
+        in_specs=[whole],
+        out_specs=(whole,) * 2,
+        scratch_shapes=[vmem((half, half), jnp.float32), vmem((half, half), jnp.float32)],
+    )(gram)
+    width = 2 * samples + 128
+    step = pl.pallas_call(
+        functools.partial(descent_kernel, layers),
+        out_shape=shaped((1, columns), jnp.float32),
+        in_specs=[whole] * 4,
+        out_specs=whole,
+        scratch_shapes=[
+            vmem((ITERS, 2 * QUAD, 1, width), jnp.float32),
+            vmem((ITERS, layers, 1, width), jnp.float32),
+            vmem((1, half), jnp.float32),
+            vmem((1, half), jnp.float32),
+            dma((ITERS, 2 * QUAD - 1)),
+            dma((ITERS, 2 * QUAD - 1)),
+            dma((ITERS, layers - 1)),
+            dma((ITERS, layers - 1)),
+            dma((1,)),
+            dma((1,)),
+        ],
+        compiler_params=pltpu.CompilerParams(collective_id=1, has_side_effects=True),
+    )(scaled, upper, lower, gradient)
+    return step[0]
+
 
 def solution(mesh):
     placed = (P("samp", "feat"), P("samp"), P("feat"), P("samp"))
+    devices, groups = mesh.shape["feat"], mesh.shape["samp"]
+    apart = groups == 2 and devices % QUAD == 0 and devices > QUAD and F // devices == 2 * BLK
     return jax.shard_map(
-        per_device, mesh=mesh, in_specs=placed, out_specs=P("feat"), check_vma=False
-    )
+        split_device if apart else per_device,
+        mesh=mesh,
+        in_specs=placed,
+        out_specs=P("feat"),
+        check_vma=False,
+    )

time: 666 us -> 135 us (0.20); the launches traced: 659 us -> 136 us
  other arithmetic: 253 us -> 0 us
  blocking collectives: 238 us -> 0 us
  Pallas kernels: 0 us -> 133 us
  matrix products: 58.7 us -> 0 us
  waiting for transfers between devices: 47 us -> 0 us
  local copies, waits for them, and re-layouts: 38.2 us -> 2.98 us
  between operations: 24.2 us -> 0.02 us
    another operation x51 -> x0, other arithmetic: 239 us -> none  [the longest x16 156 us: per_device(): factors = jnp.linalg.cholesky(gram)]
    psum x11 -> x0, blocking collectives: 238 us -> none  [the longest x3 92 us: curvature(): image_rows = lax.psum(matrix_vector(scaled, vector), 'feat')]
    pallas_call x0 -> x3, Pallas kernels: none -> 133 us  [the longest x1 64 us: split_device(): pl.pallas_call(inverse_kernel, out_shape=(shaped((half, half), jnp.bfloat...]
    psum x1 -> x0, waiting for transfers between devices: 47 us -> none  [per_device(): summed = lax.psum(partial_gram, 'samp')]
    another operation x48 -> x0, matrix products: 39.3 us -> none  [the longest x21 15 us: block_solve(): jax.scipy.linalg.solve_triangular(factor, column, lower=True, trans=1)]
    dot_general x17 -> x0, matrix products: 19.4 us -> none  [the longest x4 5.45 us: matrix_vector(): jnp.dot(matrix, lower_part, preferred_element_type=jnp.float32)]
    gather x3 -> x0, local copies, waits for them, and re-layouts: 16.4 us -> none  [the longest x2 10.3 us: per_device(): jnp.take(features, sampled, axis=0) * root_curv[:, None]]
    another operation x21 -> x0, local copies, waits for them, and re-layouts: 15.8 us -> none  [the longest x13 14.2 us: block_solve(): jax.scipy.linalg.solve_triangular(factor, column, lower=True, trans=1)]
  transfers between devices with their start and end apart: 1 -> 0, of which waited for: 1 -> 0; matrix products, arithmetic and copies ran while one was open for 1% -> 0% of each run, Pallas kernels for 0% -> 0%
where the time goes in v1:
time: 135 us; the launch traced here: 136 us
  Pallas kernels  133 us (99%)
  local copies, waits for them, and re-layouts  2.98 us (2%)
    pallas_call x1, Pallas kernels, split_device(): pl.pallas_call(inverse_kernel, out_shape=(shaped((half, half), jnp.bfloat...  64 us
    pallas_call x1, Pallas kernels, split_device(): pl.pallas_call(functools.partial(gram_kernel, layers), out_shape=(shaped(...  35.5 us
    pallas_call x1, Pallas kernels, split_device(): pl.pallas_call(functools.partial(descent_kernel, layers), out_shape=shape...  33.6 us

profile of v1, /device:TPU:0, one launch (start us, length us, event | category | flops | bytes accessed | tf_op | source)
XLA Modules:
  0.0 136.0 jit_solution(7539788860804725567)
XLA Ops:
  0.0 1.7 %copy.5.sampled = s32[1024,1]{1,0:T(8,128)} copy(s32[1024,1]{0,1:T(1,128)} %bitcast.6) | data formatting | bytes 8192 | tf_op jit(solution)/shard_map/broadcast_in_dim | solution.py:538
  1.7 35.5 %shard_map.46 = (bf16[2048,512]{1,0:T(8,128)(2,1)}, f32[512,512]{1,0:T(8,128)}, f32[1,512]{1,0:T(1,128)}) custom-call(bf16[2048,1024]{1,0:T(8,128)(2,1)} %features.1, f32[1,1024]{1,0:T(1,128)} %bitcast.7, s32[1,2048]{1,0:T(1,128)} %bitcast.5, s32[1024,1]{1,0:T(8,128)} %copy.5.sampled), custom_call_target="tpu_custom_call" | custom-call | tf_op jit(solution)/shard_map/pallas_call | solution.py:508
  37.2 64.0 %shard_map.47 = (bf16[512,512]{1,0:T(8,128)(2,1)}, bf16[512,512]{1,0:T(8,128)(2,1)}) custom-call(f32[512,512]{1,0:T(8,128)} %get-tuple-element.11.gram), custom_call_target="tpu_custom_call" | custom-call | tf_op jit(solution)/shard_map/pallas_call | solution.py:539
  101.2 33.6 %shard_map.48 = f32[1,1024]{1,0:T(1,128)} custom-call(bf16[2048,512]{1,0:T(8,128)(2,1)} %get-tuple-element.10.scaled, bf16[512,512]{1,0:T(8,128)(2,1)} %get-tuple-element.12.upper, bf16[512,512]{1,0:T(8,128)(2,1)} %get-tuple-element.13.lower, f32[1,512]{1,0:T(1,128)} %get-tuple-element.14.gradient), custom_call_target="tpu_custom_call" | custom-call | tf_op jit(solution)/shard_map/pallas_call | solution.py:547
  134.8 1.3 copy.7

commit v2 on v1

--- a/solution.py
+++ b/solution.py
@@ -237,26 +237,39 @@
 
 
 def gram_kernel(
-    layers, features, weights, labels, sampled,
+    layers, features_home, weights, labels, sampled,
     scaled, gram, gradient,
-    chosen, own_rows, sent_rows, came_rows, quad_slots, depth_slots, root_sent, root_came, grad_sent, grad_came,
-    ship_send, ship_recv, quad_send, quad_recv, depth_send, depth_recv, small_send, small_recv,
+    features, chosen, own_rows, sent_rows, came_rows, quad_slots, depth_slots, root_sent, root_came, grad_sent, grad_came,
+    load_sem, ship_send, ship_recv, quad_send, quad_recv, depth_send, depth_recv, small_send, small_recv,
 ):
     depth, quarter, samp = place()
     rows, columns = features.shape
-    samples = sampled.shape[0]
+    samples = sampled.shape[1]
     half = columns // 2
     partner = {"feat": depth * QUAD + quarter, "samp": 1 - samp}
     across = quad_peers(depth, quarter, samp)
     along = depth_peers(layers, depth, quarter, samp)
-    wait_all = greet([partner] + across + along)
     mine_at = pl.multiple_of(samp * half, 128)
     other_at = pl.multiple_of((1 - samp) * half, 128)
     piece = samples // CHUNKS
 
-    quad_slots[quarter] = row_times_transposed(weights[...], features[...])
+    def load(number, start):
+        return pltpu.make_async_copy(
+            features_home.at[:, pl.ds(start, half)],
+            features.at[:, pl.ds(start, half)],
+            load_sem.at[number],
+        )
+
+    load_other, load_mine = load(0, other_at), load(1, mine_at)
+    load_other.start()
+    load_mine.start()
+    wait_all = greet([partner] + across + along)
+    names = jnp.transpose(jnp.broadcast_to(sampled[...], (128, samples)))
+    for start in range(0, rows, 128):
+        number = lax.broadcasted_iota(jnp.int32, (samples, 128), 1) + start
+        chosen[:, start : start + 128] = jnp.where(number == names, 1.0, 0.0).astype(jnp.bfloat16)
+    load_other.wait()
     wait_all()
-    quad_copies = start_exchange(quad_slots, quarter, across, quad_send, quad_recv)
 
     def ship(number):
         first = number * piece
@@ -270,20 +283,16 @@
 
     def pick(number, carry):
         first = pl.multiple_of(number * piece, 128)
-        names = jnp.broadcast_to(sampled[pl.ds(first, piece), :], (piece, rows))
-        hot = jnp.where(lax.broadcasted_iota(jnp.int32, (piece, rows), 1) == names, 1.0, 0.0)
-        hot = hot.astype(jnp.bfloat16)
-        chosen[pl.ds(first, piece), :] = hot
-        sent_rows[pl.ds(first, piece), :] = mxu(hot, features[:, pl.ds(other_at, half)], 1, 0).astype(
-            jnp.bfloat16
-        )
+        sent_rows[pl.ds(first, piece), :] = mxu(
+            chosen[pl.ds(first, piece), :], features[:, pl.ds(other_at, half)], 1, 0
+        ).astype(jnp.bfloat16)
         ship(number).start()
         return carry
 
     lax.fori_loop(0, CHUNKS, pick, 0)
-    finish(quad_copies)
-    depth_slots[depth] = total_of(quad_slots, QUAD)
-    depth_copies = start_exchange(depth_slots, depth, along, depth_send, depth_recv)
+    load_mine.wait()
+    quad_slots[quarter] = row_times_transposed(weights[...], features[...])
+    quad_copies = start_exchange(quad_slots, quarter, across, quad_send, quad_recv)
 
     def pick_own(number, carry):
         first = pl.multiple_of(number * piece, 128)
@@ -292,6 +301,9 @@
         ).astype(jnp.bfloat16)
         return carry
 
+    finish(quad_copies)
+    depth_slots[depth] = total_of(quad_slots, QUAD)
+    depth_copies = start_exchange(depth_slots, depth, along, depth_send, depth_recv)
     lax.fori_loop(0, CHUNKS, pick_own, 0)
     finish(depth_copies)
     margin = total_of(depth_slots, layers)
@@ -307,39 +319,42 @@
     grad_copy.start()
     own_grad = row_times(residue, features[:, pl.ds(mine_at, half)])
 
-    def scale_into(source, root_row, start):
-        factor = jnp.transpose(jnp.broadcast_to(root_row, (128, samples)))
+    def scale_into(source, factor, first, start):
         for column in range(0, half, 128):
-            wide = source[:, column : column + 128].astype(jnp.float32) * factor
-            scaled[pl.ds(start, samples), column : column + 128] = wide.astype(jnp.bfloat16)
+            wide = source[pl.ds(first, piece), column : column + 128].astype(jnp.float32) * factor
+            scaled[pl.ds(start, piece), column : column + 128] = wide.astype(jnp.bfloat16)
+
+    def root_factor(root_row, number):
+        part = root_row[:, number * piece : (number + 1) * piece]
+        return jnp.transpose(jnp.broadcast_to(part, (128, piece)))
 
     mine_row = pl.multiple_of(samp * samples, 128)
     other_row = pl.multiple_of((1 - samp) * samples, 128)
-    scale_into(own_rows, own_root, mine_row)
+    for number in range(CHUNKS):
+        first = number * piece
+        scale_into(own_rows, root_factor(own_root, number), first, mine_row + first)
     own_block = scaled[pl.ds(mine_row, samples), :]
     gram[...] = mxu(own_block, own_block, 0, 0)
-
-    def settle(number, carry):
+    for number in range(CHUNKS):
+        first = number * piece
         ship(number).wait()
-        return carry
-
-    root_copy.wait()
+        if number == 0:
+            root_copy.wait()
+        scale_into(came_rows, root_factor(root_came[...], number), first, other_row + first)
+        block = scaled[pl.ds(other_row + first, piece), :]
+        gram[...] += mxu(block, block, 0, 0)
+    ridge_term = RIDGE_COEF / F
+    diagonal = lax.broadcasted_iota(jnp.int32, gram.shape, 0) == lax.broadcasted_iota(
+        jnp.int32, gram.shape, 1
+    )
+    gram[...] = gram[...] / (2 * samples) + jnp.where(diagonal, ridge_term, 0.0)
     grad_copy.wait()
-    ridge_term = RIDGE_COEF / F
     gradient[...] = (own_grad + grad_came[...]) / (2 * rows) + ridge_term * weights[
         :, pl.ds(mine_at, half)
     ]
-    lax.fori_loop(0, CHUNKS, settle, 0)
-    scale_into(came_rows, root_came[...], other_row)
-    other_block = scaled[pl.ds(other_row, samples), :]
-    both = gram[...] + mxu(other_block, other_block, 0, 0)
-    diagonal = lax.broadcasted_iota(jnp.int32, both.shape, 0) == lax.broadcasted_iota(
-        jnp.int32, both.shape, 1
-    )
-    gram[...] = both / (2 * samples) + jnp.where(diagonal, ridge_term, 0.0)
-
-
-SQUARINGS = 8
+
+
+SQUARINGS = 6
 POLISH = 2
 LIMIT = 60
 
@@ -349,7 +364,7 @@
     return top, (value - top.astype(jnp.float32)).astype(jnp.bfloat16)
 
 
-def inverse_kernel(gram, upper, lower, unit, inverse):
+def inverse_kernel(gram, upper, lower, unit, inverse, pair):
     order = gram.shape[0]
     bound = jnp.max(jnp.sum(jnp.abs(gram[...]), axis=0, keepdims=True))
     shape = (order, order)
@@ -363,14 +378,20 @@
     power = eye - normed
     inverse[...] = eye + power
 
-    def square(_, power_now):
-        squared = mxu(power_now, power_now, 1, 0)
-        power_next = squared.astype(jnp.bfloat16)
-        value = inverse[...]
-        inverse[...] = value + mxu(value.astype(jnp.bfloat16), power_next, 1, 0)
-        return power_next
-
-    lax.fori_loop(0, SQUARINGS, square, power.astype(jnp.bfloat16))
+    first = power.astype(jnp.bfloat16)
+    pair[:order] = mxu(first, first, 1, 0).astype(jnp.bfloat16)
+    pair[order:] = inverse[...].astype(jnp.bfloat16)
+
+    def square(_, carry):
+        product = mxu(pair[...], pair[:order], 1, 0)
+        value = inverse[...] + product[order:]
+        inverse[...] = value
+        pair[:order] = product[:order].astype(jnp.bfloat16)
+        pair[order:] = value.astype(jnp.bfloat16)
+        return carry
+
+    lax.fori_loop(0, SQUARINGS - 1, square, 0)
+    inverse[...] += mxu(pair[order:], pair[:order], 1, 0)
     unit_top, unit_low = halves(unit[...])
 
     def polish(_, size):
@@ -512,9 +533,10 @@
             shaped((half, half), jnp.float32),
             shaped((1, half), jnp.float32),
         ),
-        in_specs=[whole] * 4,
+        in_specs=[pl.BlockSpec(memory_space=pl.ANY)] + [whole] * 3,
         out_specs=(whole,) * 3,
         scratch_shapes=[
+            vmem((rows, columns), jnp.bfloat16),
             vmem((samples, rows), jnp.bfloat16),
             vmem((samples, half), jnp.bfloat16),
             vmem((samples, half), jnp.bfloat16),
@@ -525,6 +547,7 @@
             vmem((1, samples), jnp.float32),
             vmem((1, half), jnp.float32),
             vmem((1, half), jnp.float32),
+            dma((2,)),
             dma((CHUNKS,)),
             dma((CHUNKS,)),
             dma((QUAD - 1,)),
@@ -535,13 +558,17 @@
             dma((2,)),
         ],
         compiler_params=pltpu.CompilerParams(collective_id=0, has_side_effects=True),
-    )(features, weights[None, :], labels[None, :], sampled[:, None])
+    )(features, weights[None, :], labels[None, :], sampled[None, :])
     upper, lower = pl.pallas_call(
         inverse_kernel,
         out_shape=(shaped((half, half), jnp.bfloat16),) * 2,
         in_specs=[whole],
         out_specs=(whole,) * 2,
-        scratch_shapes=[vmem((half, half), jnp.float32), vmem((half, half), jnp.float32)],
+        scratch_shapes=[
+            vmem((half, half), jnp.float32),
+            vmem((half, half), jnp.float32),
+            vmem((2 * half, half), jnp.bfloat16),
+        ],
     )(gram)
     width = 2 * samples + 128
     step = pl.pallas_call(

time: 135 us -> 130 us (0.963); the launches traced: 136 us -> 128 us
  Pallas kernels: 133 us -> 127 us
  local copies, waits for them, and re-layouts: 2.98 us -> 1.28 us
    pallas_call x1, Pallas kernels: 33.6 us -> 31.2 us  [split_device(): pl.pallas_call(functools.partial(descent_kernel, layers), out_shape=shape...]
    pallas_call x1, Pallas kernels: 64 us -> 61.6 us  [split_device(): pl.pallas_call(inverse_kernel, out_shape=(shaped((half, half), jnp.bfloat...]
    broadcast_in_dim x1 -> x0, local copies, waits for them, and re-layouts: 1.7 us -> none  [split_device(): sampled[:, None]]
where the time goes in v2:
time: 130 us; the launch traced here: 128 us
  Pallas kernels  127 us (98%)
    pallas_call x1, Pallas kernels, split_device(): pl.pallas_call(inverse_kernel, out_shape=(shaped((half, half), jnp.bfloat...  61.6 us
    pallas_call x1, Pallas kernels, split_device(): pl.pallas_call(functools.partial(gram_kernel, layers), out_shape=(shaped(...  34.3 us
    pallas_call x1, Pallas kernels, split_device(): pl.pallas_call(functools.partial(descent_kernel, layers), out_shape=shape...  31.2 us

profile of v2, /device:TPU:0, one launch (start us, length us, event | category | flops | bytes accessed | tf_op | source)
XLA Modules:
  0.0 128.4 jit_solution(3886113164041682791)
XLA Ops:
  0.0 34.3 %shard_map.46 = (bf16[2048,512]{1,0:T(8,128)(2,1)}, f32[512,512]{1,0:T(8,128)}, f32[1,512]{1,0:T(1,128)}) custom-call(bf16[2048,1024]{1,0:T(8,128)(2,1)} %features_home.1, f32[1,1024]{1,0:T(1,128)} %bitcast.6, s32[1,2048]{1,0:T(1,128)} %bitcast.5, s32[1,1024]{1,0:T(1,128)} %bitcast.7), custom_call_target="tpu_custom_call" | custom-call | tf_op jit(solution)/shard_map/pallas_call | solution.py:529
  34.3 61.6 %shard_map.47 = (bf16[512,512]{1,0:T(8,128)(2,1)}, bf16[512,512]{1,0:T(8,128)(2,1)}) custom-call(f32[512,512]{1,0:T(8,128)} %get-tuple-element.11.gram), custom_call_target="tpu_custom_call" | custom-call | tf_op jit(solution)/shard_map/pallas_call | solution.py:562
  95.9 31.2 %shard_map.48 = f32[1,1024]{1,0:T(1,128)} custom-call(bf16[2048,512]{1,0:T(8,128)(2,1)} %get-tuple-element.10.scaled, bf16[512,512]{1,0:T(8,128)(2,1)} %get-tuple-element.12.upper, bf16[512,512]{1,0:T(8,128)(2,1)} %get-tuple-element.13.lower, f32[1,512]{1,0:T(1,128)} %get-tuple-element.14.gradient), custom_call_target="tpu_custom_call" | custom-call | tf_op jit(solution)/shard_map/pallas_call | solution.py:574
  127.1 1.3 copy.6

commit v3 on v2

--- a/solution.py
+++ b/solution.py
@@ -238,9 +238,9 @@
 
 def gram_kernel(
     layers, features_home, weights, labels, sampled,
-    scaled, gram, gradient,
-    features, chosen, own_rows, sent_rows, came_rows, quad_slots, depth_slots, root_sent, root_came, grad_sent, grad_came,
-    load_sem, ship_send, ship_recv, quad_send, quad_recv, depth_send, depth_recv, small_send, small_recv,
+    scaled_home, gram_home, gradient, upper, lower, size,
+    scaled, gram, inverse, pair, features, chosen, own_rows, sent_rows, came_rows, quad_slots, depth_slots, root_sent, root_came, grad_sent, grad_came,
+    load_sem, store_sem, ship_send, ship_recv, quad_send, quad_recv, depth_send, depth_recv, small_send, small_recv,
 ):
     depth, quarter, samp = place()
     rows, columns = features.shape
@@ -333,30 +333,56 @@
     for number in range(CHUNKS):
         first = number * piece
         scale_into(own_rows, root_factor(own_root, number), first, mine_row + first)
+    stores = [
+        pltpu.make_async_copy(
+            scaled.at[pl.ds(mine_row, samples)],
+            scaled_home.at[pl.ds(mine_row, samples)],
+            store_sem.at[CHUNKS],
+        )
+    ]
+    stores[0].start()
     own_block = scaled[pl.ds(mine_row, samples), :]
     gram[...] = mxu(own_block, own_block, 0, 0)
+    ridge_term = RIDGE_COEF / F
+    shape = gram.shape
+    same = lax.broadcasted_iota(jnp.int32, shape, 0) == lax.broadcasted_iota(jnp.int32, shape, 1)
+    eye = jnp.where(same, 1.0, 0.0)
+    bound = None
     for number in range(CHUNKS):
         first = number * piece
+        if number == CHUNKS - 1:
+            bound = early_inverse(gram[...] / (samples + first) + ridge_term * eye, eye, inverse, pair)
         ship(number).wait()
         if number == 0:
             root_copy.wait()
         scale_into(came_rows, root_factor(root_came[...], number), first, other_row + first)
+        store = pltpu.make_async_copy(
+            scaled.at[pl.ds(other_row + first, piece)],
+            scaled_home.at[pl.ds(other_row + first, piece)],
+            store_sem.at[number],
+        )
+        store.start()
+        stores.append(store)
         block = scaled[pl.ds(other_row + first, piece), :]
         gram[...] += mxu(block, block, 0, 0)
-    ridge_term = RIDGE_COEF / F
-    diagonal = lax.broadcasted_iota(jnp.int32, gram.shape, 0) == lax.broadcasted_iota(
-        jnp.int32, gram.shape, 1
-    )
-    gram[...] = gram[...] / (2 * samples) + jnp.where(diagonal, ridge_term, 0.0)
+    gram[...] = gram[...] / (2 * samples) + ridge_term * eye
+    store = pltpu.make_async_copy(gram, gram_home, store_sem.at[CHUNKS + 1])
+    store.start()
+    stores.append(store)
+    size[...] = jnp.broadcast_to(late_inverse(gram, bound, eye, inverse, pair, upper, lower), (1, 128))
     grad_copy.wait()
     gradient[...] = (own_grad + grad_came[...]) / (2 * rows) + ridge_term * weights[
         :, pl.ds(mine_at, half)
     ]
+    for store in stores:
+        store.wait()
 
 
 SQUARINGS = 6
 POLISH = 2
 LIMIT = 60
+DAMP = 0.75
+SETTLED = 0.0025
 
 
 def halves(value):
@@ -364,23 +390,8 @@
     return top, (value - top.astype(jnp.float32)).astype(jnp.bfloat16)
 
 
-def inverse_kernel(gram, upper, lower, unit, inverse, pair):
-    order = gram.shape[0]
-    bound = jnp.max(jnp.sum(jnp.abs(gram[...]), axis=0, keepdims=True))
-    shape = (order, order)
-    eye = jnp.where(
-        lax.broadcasted_iota(jnp.int32, shape, 0) == lax.broadcasted_iota(jnp.int32, shape, 1),
-        1.0,
-        0.0,
-    )
-    normed = gram[...] / bound
-    unit[...] = normed
-    power = eye - normed
-    inverse[...] = eye + power
-
-    first = power.astype(jnp.bfloat16)
-    pair[:order] = mxu(first, first, 1, 0).astype(jnp.bfloat16)
-    pair[order:] = inverse[...].astype(jnp.bfloat16)
+def raise_power(inverse, pair, count):
+    order = inverse.shape[0]
 
     def square(_, carry):
         product = mxu(pair[...], pair[:order], 1, 0)
@@ -390,23 +401,59 @@
         pair[order:] = value.astype(jnp.bfloat16)
         return carry
 
-    lax.fori_loop(0, SQUARINGS - 1, square, 0)
+    lax.fori_loop(0, count - 1, square, 0)
     inverse[...] += mxu(pair[order:], pair[:order], 1, 0)
-    unit_top, unit_low = halves(unit[...])
-
-    def polish(_, size):
+
+
+def early_inverse(early, eye, inverse, pair):
+    order = early.shape[0]
+    bound = jnp.max(jnp.sum(jnp.abs(early), axis=0, keepdims=True), axis=1, keepdims=True)
+    power = eye - early / bound
+    value = eye + power
+    inverse[...] = value
+    first = power.astype(jnp.bfloat16)
+    pair[:order] = mxu(first, first, 1, 0).astype(jnp.bfloat16)
+    pair[order:] = value.astype(jnp.bfloat16)
+    raise_power(inverse, pair, SQUARINGS)
+    return bound
+
+
+def late_inverse(gram, bound, eye, inverse, pair, upper, lower):
+    order = gram.shape[0]
+    unit_top, unit_low = halves(gram[...] / bound)
+    value = DAMP * inverse[...]
+    inverse[...] = value
+    top = value.astype(jnp.bfloat16)
+    pair[order:] = top
+    pair[:order] = (eye - mxu(unit_top, top, 1, 0)).astype(jnp.bfloat16)
+    raise_power(inverse, pair, 2)
+    left = None
+    for _ in range(POLISH):
         value = inverse[...]
         top, low = halves(value)
         product = mxu(unit_top, top, 1, 0) + mxu(unit_top, low, 1, 0) + mxu(unit_low, top, 1, 0)
         left = eye - product
         inverse[...] = value + mxu(top, left.astype(jnp.bfloat16), 1, 0)
-        return jnp.sum(left * left)
-
-    size = lax.fori_loop(0, POLISH, polish, jnp.float32(0.0))
-    settled = size < 0.0025
+    top, low = halves(inverse[...] / bound)
+    upper[...] = top
+    lower[...] = low
+    return jnp.sum(jnp.sum(left * left, axis=0, keepdims=True), axis=1, keepdims=True)
+
+
+def rescue_kernel(size, gram_home, _upper, _lower, upper_home, lower_home, unit, inverse, top_half, low_half):
+    settled = size[0, 0] < SETTLED
 
     @pl.when(jnp.logical_not(settled))
     def _():
+        pltpu.sync_copy(gram_home, unit)
+        bound = jnp.max(jnp.sum(jnp.abs(unit[...]), axis=0, keepdims=True))
+        unit[...] = unit[...] / bound
+        shape = unit.shape
+        eye = jnp.where(
+            lax.broadcasted_iota(jnp.int32, shape, 0) == lax.broadcasted_iota(jnp.int32, shape, 1),
+            1.0,
+            0.0,
+        )
         inverse[...] = eye
 
         def exact(left, right):
@@ -427,23 +474,26 @@
             return count + 1, jnp.sum(left * left)
 
         lax.while_loop(going, step, (jnp.int32(0), jnp.float32(1.0)))
-
-    top, low = halves(inverse[...] / bound)
-    upper[...] = top
-    lower[...] = low
+        top, low = halves(inverse[...] / bound)
+        top_half[...] = top
+        low_half[...] = low
+        pltpu.sync_copy(top_half, upper_home)
+        pltpu.sync_copy(low_half, lower_home)
 
 
 def descent_kernel(
-    layers, scaled, upper, lower, gradient,
+    layers, scaled_home, upper, lower, gradient,
     step,
-    plane_slots, depth_slots, last_sent, last_came,
-    plane_send, plane_recv, depth_send, depth_recv, last_send, last_recv,
+    scaled, plane_slots, depth_slots, part_sent, part_came,
+    load_sem, plane_send, plane_recv, depth_send, depth_recv, part_send, part_recv,
 ):
     depth, quarter, samp = place()
     samples, half = scaled.shape
     partner = {"feat": depth * QUAD + quarter, "samp": 1 - samp}
     plane = plane_peers(depth, quarter, samp)
     along = depth_peers(layers, depth, quarter, samp)
+    load = pltpu.make_async_copy(scaled_home, scaled, load_sem.at[0])
+    load.start()
     wait_all = greet(plane + along)
     member = samp * QUAD + quarter
     ridge_term = RIDGE_COEF / F
@@ -459,6 +509,8 @@
     residual = -gradient[...]
     answer = jnp.zeros_like(residual)
     direction = jnp.zeros_like(residual)
+    twin_answer = jnp.zeros_like(residual)
+    twin_direction = jnp.zeros_like(residual)
     along_rows = None
     rz_now = None
     length = None
@@ -474,21 +526,33 @@
             ),
         )
         mine = plane_slots.at[iteration, member]
+        part_sent[iteration] = precond
+        if iteration == 0:
+            load.wait()
         mine[:, :samples] = row_times_transposed(precond, scaled[...])
         mine[:, samples:] = numbers
         if iteration == 0:
             wait_all()
-        finish(
-            start_exchange(
-                plane_slots.at[iteration], member, plane, plane_send.at[iteration], plane_recv.at[iteration]
-            )
-        )
+        plane_copies = start_exchange(
+            plane_slots.at[iteration], member, plane, plane_send.at[iteration], plane_recv.at[iteration]
+        )
+        twin_copy = remote(
+            part_sent.at[iteration],
+            part_came.at[iteration],
+            part_send.at[iteration],
+            part_recv.at[iteration],
+            partner,
+        )
+        twin_copy.start()
+        finish(plane_copies)
         depth_slots[iteration, depth] = total_of(plane_slots.at[iteration], 2 * QUAD)
         finish(
             start_exchange(
                 depth_slots.at[iteration], depth, along, depth_send.at[iteration], depth_recv.at[iteration]
             )
         )
+        twin_copy.wait()
+        twin_precond = part_came[iteration]
         summed = total_of(depth_slots.at[iteration], layers)
         image_rows = summed[:, :samples]
         fresh = summed[:, samples : samples + 1]
@@ -496,25 +560,24 @@
         cross = summed[:, samples + 2 : samples + 3]
         if iteration == 0:
             direction = precond
+            twin_direction = twin_precond
             along_rows = image_rows
             length = square
         else:
             beta = fresh / rz_now
             direction = precond + beta * direction
+            twin_direction = twin_precond + beta * twin_direction
             along_rows = image_rows + beta * along_rows
             length = square + 2.0 * beta * cross + beta * beta * length
         rz_now = fresh
         alpha = rz_now / (total(along_rows * along_rows) / samples + ridge_term * length)
         answer = answer + alpha * direction
+        twin_answer = twin_answer + alpha * twin_direction
         if iteration + 1 < ITERS:
             image = row_times(along_rows, scaled[...]) / samples + ridge_term * direction
             residual = residual - alpha * image
-    last_sent[...] = answer
-    final = remote(last_sent, last_came, last_send.at[0], last_recv.at[0], partner)
-    final.start()
     step[:, pl.ds(pl.multiple_of(samp * half, 128), half)] = answer
-    final.wait()
-    step[:, pl.ds(pl.multiple_of((1 - samp) * half, 128), half)] = last_came[...]
+    step[:, pl.ds(pl.multiple_of((1 - samp) * half, 128), half)] = twin_answer
 
 
 def split_device(features, labels, weights, sampled):
@@ -526,16 +589,24 @@
     whole = pl.BlockSpec(memory_space=pltpu.VMEM)
     dma = pltpu.SemaphoreType.DMA
     vmem = pltpu.VMEM
-    scaled, gram, gradient = pl.pallas_call(
+    anywhere = pl.BlockSpec(memory_space=pl.ANY)
+    scaled, gram, gradient, upper, lower, size = pl.pallas_call(
         functools.partial(gram_kernel, layers),
         out_shape=(
             shaped((2 * samples, half), jnp.bfloat16),
             shaped((half, half), jnp.float32),
             shaped((1, half), jnp.float32),
+            shaped((half, half), jnp.bfloat16),
+            shaped((half, half), jnp.bfloat16),
+            shaped((1, 128), jnp.float32),
         ),
-        in_specs=[pl.BlockSpec(memory_space=pl.ANY)] + [whole] * 3,
-        out_specs=(whole,) * 3,
+        in_specs=[anywhere] + [whole] * 3,
+        out_specs=(anywhere,) * 2 + (whole,) * 4,
         scratch_shapes=[
+            vmem((2 * samples, half), jnp.bfloat16),
+            vmem((half, half), jnp.float32),
+            vmem((half, half), jnp.float32),
+            vmem((2 * half, half), jnp.bfloat16),
             vmem((rows, columns), jnp.bfloat16),
             vmem((samples, rows), jnp.bfloat16),
             vmem((samples, half), jnp.bfloat16),
@@ -548,6 +619,7 @@
             vmem((1, half), jnp.float32),
             vmem((1, half), jnp.float32),
             dma((2,)),
+            dma((CHUNKS + 2,)),
             dma((CHUNKS,)),
             dma((CHUNKS,)),
             dma((QUAD - 1,)),
@@ -560,33 +632,37 @@
         compiler_params=pltpu.CompilerParams(collective_id=0, has_side_effects=True),
     )(features, weights[None, :], labels[None, :], sampled[None, :])
     upper, lower = pl.pallas_call(
-        inverse_kernel,
+        rescue_kernel,
         out_shape=(shaped((half, half), jnp.bfloat16),) * 2,
-        in_specs=[whole],
-        out_specs=(whole,) * 2,
+        in_specs=[pl.BlockSpec(memory_space=pltpu.SMEM)] + [anywhere] * 3,
+        out_specs=(anywhere,) * 2,
         scratch_shapes=[
             vmem((half, half), jnp.float32),
             vmem((half, half), jnp.float32),
-            vmem((2 * half, half), jnp.bfloat16),
+            vmem((half, half), jnp.bfloat16),
+            vmem((half, half), jnp.bfloat16),
         ],
-    )(gram)
+        input_output_aliases={2: 0, 3: 1},
+    )(size, gram, upper, lower)
     width = 2 * samples + 128
     step = pl.pallas_call(
         functools.partial(descent_kernel, layers),
         out_shape=shaped((1, columns), jnp.float32),
-        in_specs=[whole] * 4,
+        in_specs=[anywhere] + [whole] * 3,
         out_specs=whole,
         scratch_shapes=[
+            vmem((2 * samples, half), jnp.bfloat16),
             vmem((ITERS, 2 * QUAD, 1, width), jnp.float32),
             vmem((ITERS, layers, 1, width), jnp.float32),
-            vmem((1, half), jnp.float32),
-            vmem((1, half), jnp.float32),
+            vmem((ITERS, 1, half), jnp.float32),
+            vmem((ITERS, 1, half), jnp.float32),
+            dma((1,)),
             dma((ITERS, 2 * QUAD - 1)),
             dma((ITERS, 2 * QUAD - 1)),
             dma((ITERS, layers - 1)),
             dma((ITERS, layers - 1)),
-            dma((1,)),
-            dma((1,)),
+            dma((ITERS,)),
+            dma((ITERS,)),
         ],
         compiler_params=pltpu.CompilerParams(collective_id=1, has_side_effects=True),
     )(scaled, upper, lower, gradient)

time: 130 us -> 131 us (level); the launches traced: 128 us -> 131 us
  Pallas kernels: 127 us -> 130 us
    pallas_call x1, Pallas kernels: 34.3 us -> 42.2 us  [split_device(): pl.pallas_call(functools.partial(gram_kernel, layers), out_shape=(shaped(...]
    pallas_call x1, Pallas kernels: 61.6 us -> 55.6 us  [split_device(): pl.pallas_call(rescue_kernel, out_shape=(shaped((half, half), jnp.bfloat1...]
where the time goes in v3:
time: 131 us
  Pallas kernels  130 us (99%)
    pallas_call x1, Pallas kernels, split_device(): pl.pallas_call(rescue_kernel, out_shape=(shaped((half, half), jnp.bfloat1...  55.6 us
    pallas_call x1, Pallas kernels, split_device(): pl.pallas_call(functools.partial(gram_kernel, layers), out_shape=(shaped(...  42.2 us
    pallas_call x1, Pallas kernels, split_device(): pl.pallas_call(functools.partial(descent_kernel, layers), out_shape=shape...  32 us

profile of v3, /device:TPU:0, one launch (start us, length us, event | category | flops | bytes accessed | tf_op | source)
XLA Modules:
  0.0 131.1 jit_solution(3566291290076818217)
XLA Ops:
  0.0 42.2 %shard_map.46 = (bf16[2048,512]{1,0:T(8,128)(2,1)}, f32[512,512]{1,0:T(8,128)}, f32[1,512]{1,0:T(1,128)}, bf16[512,512]{1,0:T(8,128)(2,1)}, bf16[512,512]{1,0:T(8,128)(2,1)}, /*index=5*/f32[1,128]{1,0:T(1,128)}) custom-call(bf16[2048,1024]{1,0:T(8,128)(2,1)} %features_home.1, f32[1,1024]{1,0:T(1,128)} %bitcast.6, s32[1,2048]{1,0:T(1,128)} %bitcast.5, ...), custom_call_target="tpu_custom_call" | custom-call | tf_op jit(solution)/shard_map/pallas_call | solution.py:593
  42.2 55.6 %shard_map.47 = (bf16[512,512]{1,0:T(8,128)(2,1)}, bf16[512,512]{1,0:T(8,128)(2,1)}) custom-call(f32[1,128]{1,0:T(1,128)} %get-tuple-element.14.size, f32[512,512]{1,0:T(8,128)} %get-tuple-element.15.gram_home, bf16[512,512]{1,0:T(8,128)(2,1)} %get-tuple-element.16._upper, ...), custom_call_target="tpu_custom_call", output_to_operand_aliasing={{0}: (2, {}), {1}: (3, {})} | custom-call | tf_op jit(solution)/shard_map/pallas_call | solution.py:634
  97.8 32.0 %shard_map.48 = f32[1,1024]{1,0:T(1,128)} custom-call(bf16[2048,512]{1,0:T(8,128)(2,1)} %get-tuple-element.13.scaled_home, bf16[512,512]{1,0:T(8,128)(2,1)} %get-tuple-element.18.upper, bf16[512,512]{1,0:T(8,128)(2,1)} %get-tuple-element.19.lower, f32[1,512]{1,0:T(1,128)} %get-tuple-element.20.gradient), custom_call_target="tpu_custom_call" | custom-call | tf_op jit(solution)/shard_map/pallas_call | solution.py:648
  129.9 1.3 copy.10

commit v4 on v3

--- a/solution.py
+++ b/solution.py
@@ -265,11 +265,13 @@
     load_mine.start()
     wait_all = greet([partner] + across + along)
     names = jnp.transpose(jnp.broadcast_to(sampled[...], (128, samples)))
-    for start in range(0, rows, 128):
-        number = lax.broadcasted_iota(jnp.int32, (samples, 128), 1) + start
-        chosen[:, start : start + 128] = jnp.where(number == names, 1.0, 0.0).astype(jnp.bfloat16)
-    load_other.wait()
-    wait_all()
+
+    def choose(first):
+        wanted = names[first : first + piece]
+        lane = lax.broadcasted_iota(jnp.int32, wanted.shape, 1)
+        for start in range(0, rows, 128):
+            hot = jnp.where(lane + start == wanted, 1.0, 0.0)
+            chosen[first : first + piece, start : start + 128] = hot.astype(jnp.bfloat16)
 
     def ship(number):
         first = number * piece
@@ -281,15 +283,17 @@
             partner,
         )
 
-    def pick(number, carry):
-        first = pl.multiple_of(number * piece, 128)
+    for number in range(CHUNKS):
+        first = number * piece
+        choose(first)
+        if number == 0:
+            load_other.wait()
         sent_rows[pl.ds(first, piece), :] = mxu(
             chosen[pl.ds(first, piece), :], features[:, pl.ds(other_at, half)], 1, 0
         ).astype(jnp.bfloat16)
+        if number == 0:
+            wait_all()
         ship(number).start()
-        return carry
-
-    lax.fori_loop(0, CHUNKS, pick, 0)
     load_mine.wait()
     quad_slots[quarter] = row_times_transposed(weights[...], features[...])
     quad_copies = start_exchange(quad_slots, quarter, across, quad_send, quad_recv)
@@ -378,11 +382,11 @@
         store.wait()
 
 
-SQUARINGS = 6
+SQUARINGS = 5
 POLISH = 2
 LIMIT = 60
-DAMP = 0.75
-SETTLED = 0.0025
+DAMP = 0.6
+SETTLED = 0.02
 
 
 def halves(value):
@@ -407,12 +411,18 @@
 
 def early_inverse(early, eye, inverse, pair):
     order = early.shape[0]
-    bound = jnp.max(jnp.sum(jnp.abs(early), axis=0, keepdims=True), axis=1, keepdims=True)
-    power = eye - early / bound
-    value = eye + power
+    norm = lambda matrix: jnp.max(
+        jnp.sum(jnp.abs(matrix), axis=0, keepdims=True), axis=1, keepdims=True
+    )
+    first_bound = norm(early)
+    first = (early / first_bound).astype(jnp.bfloat16)
+    squared = mxu(first, first, 1, 0)
+    ratio = jnp.sqrt(norm(squared))
+    bound = first_bound * ratio
+    unit = early / bound
+    value = 2.0 * eye - unit
     inverse[...] = value
-    first = power.astype(jnp.bfloat16)
-    pair[:order] = mxu(first, first, 1, 0).astype(jnp.bfloat16)
+    pair[:order] = (eye - 2.0 * unit + squared / (ratio * ratio)).astype(jnp.bfloat16)
     pair[order:] = value.astype(jnp.bfloat16)
     raise_power(inverse, pair, SQUARINGS)
     return bound

time: 131 us -> 129 us (0.985); the launches traced: 131 us -> 127 us
  Pallas kernels: 130 us -> 126 us
    pallas_call x1, Pallas kernels: 32 us -> 28.8 us  [split_device(): pl.pallas_call(functools.partial(descent_kernel, layers), out_shape=shape...]
where the time goes in v4:
time: 129 us; the launch traced here: 127 us
  Pallas kernels  126 us (98%)
    pallas_call x1, Pallas kernels, split_device(): pl.pallas_call(rescue_kernel, out_shape=(shaped((half, half), jnp.bfloat1...  55.6 us
    pallas_call x1, Pallas kernels, split_device(): pl.pallas_call(functools.partial(gram_kernel, layers), out_shape=(shaped(...  41.3 us
    pallas_call x1, Pallas kernels, split_device(): pl.pallas_call(functools.partial(descent_kernel, layers), out_shape=shape...  28.8 us

profile of v4, /device:TPU:0, one launch (start us, length us, event | category | flops | bytes accessed | tf_op | source)
XLA Modules:
  0.0 127.0 jit_solution(18215523240810467002)
XLA Ops:
  0.0 41.3 %shard_map.46 = (bf16[2048,512]{1,0:T(8,128)(2,1)}, f32[512,512]{1,0:T(8,128)}, f32[1,512]{1,0:T(1,128)}, bf16[512,512]{1,0:T(8,128)(2,1)}, bf16[512,512]{1,0:T(8,128)(2,1)}, /*index=5*/f32[1,128]{1,0:T(1,128)}) custom-call(bf16[2048,1024]{1,0:T(8,128)(2,1)} %features_home.1, f32[1,1024]{1,0:T(1,128)} %bitcast.6, s32[1,2048]{1,0:T(1,128)} %bitcast.5, ...), custom_call_target="tpu_custom_call" | custom-call | tf_op jit(solution)/shard_map/pallas_call | solution.py:603
  41.3 55.6 %shard_map.47 = (bf16[512,512]{1,0:T(8,128)(2,1)}, bf16[512,512]{1,0:T(8,128)(2,1)}) custom-call(f32[1,128]{1,0:T(1,128)} %get-tuple-element.14.size, f32[512,512]{1,0:T(8,128)} %get-tuple-element.15.gram_home, bf16[512,512]{1,0:T(8,128)(2,1)} %get-tuple-element.16._upper, ...), custom_call_target="tpu_custom_call", output_to_operand_aliasing={{0}: (2, {}), {1}: (3, {})} | custom-call | tf_op jit(solution)/shard_map/pallas_call | solution.py:644
  97.0 28.8 %shard_map.48 = f32[1,1024]{1,0:T(1,128)} custom-call(bf16[2048,512]{1,0:T(8,128)(2,1)} %get-tuple-element.13.scaled_home, bf16[512,512]{1,0:T(8,128)(2,1)} %get-tuple-element.18.upper, bf16[512,512]{1,0:T(8,128)(2,1)} %get-tuple-element.19.lower, f32[1,512]{1,0:T(1,128)} %get-tuple-element.20.gradient), custom_call_target="tpu_custom_call" | custom-call | tf_op jit(solution)/shard_map/pallas_call | solution.py:658
  125.7 1.3 %copy.10 = f32[1024]{0:T(1024)} copy(f32[1024]{0:T(1024)} %bitcast.4) | data formatting | bytes 8192

commit v5 on v4

--- a/solution.py
+++ b/solution.py
@@ -234,6 +234,7 @@
 
 
 CHUNKS = 4
+AHEAD = 2
 
 
 def gram_kernel(
@@ -293,7 +294,8 @@
         ).astype(jnp.bfloat16)
         if number == 0:
             wait_all()
-        ship(number).start()
+        if number < AHEAD:
+            ship(number).start()
     load_mine.wait()
     quad_slots[quarter] = row_times_transposed(weights[...], features[...])
     quad_copies = start_exchange(quad_slots, quarter, across, quad_send, quad_recv)
@@ -317,6 +319,8 @@
     root_sent[...] = own_root
     root_copy = remote(root_sent, root_came, small_send.at[0], small_recv.at[0], partner)
     root_copy.start()
+    for number in range(AHEAD, CHUNKS):
+        ship(number).start()
     residue = probability - labels[...].astype(jnp.float32)
     grad_sent[...] = row_times(residue, features[:, pl.ds(other_at, half)])
     grad_copy = remote(grad_sent, grad_came, small_send.at[1], small_recv.at[1], partner)

time: 129 us -> 125 us (0.969)
  Pallas kernels: 126 us -> 123 us
    pallas_call x1, Pallas kernels: 41.3 us -> 36.4 us  [split_device(): pl.pallas_call(functools.partial(gram_kernel, layers), out_shape=(shaped(...]
    pallas_call x1, Pallas kernels: 28.8 us -> 31 us  [split_device(): pl.pallas_call(functools.partial(descent_kernel, layers), out_shape=shape...]
where the time goes in v5:
time: 125 us; the launch traced here: 124 us
  Pallas kernels  123 us (98%)
  local copies, waits for them, and re-layouts  1.28 us (1%)
    pallas_call x1, Pallas kernels, split_device(): pl.pallas_call(rescue_kernel, out_shape=(shaped((half, half), jnp.bfloat1...  55.6 us
    pallas_call x1, Pallas kernels, split_device(): pl.pallas_call(functools.partial(gram_kernel, layers), out_shape=(shaped(...  36.4 us
    pallas_call x1, Pallas kernels, split_device(): pl.pallas_call(functools.partial(descent_kernel, layers), out_shape=shape...  31 us

profile of v5, /device:TPU:0, one launch (start us, length us, event | category | flops | bytes accessed | tf_op | source)
XLA Modules:
  0.0 124.3 jit_solution(346183974845386829)
XLA Ops:
  0.0 36.4 %shard_map.46 = (bf16[2048,512]{1,0:T(8,128)(2,1)}, f32[512,512]{1,0:T(8,128)}, f32[1,512]{1,0:T(1,128)}, bf16[512,512]{1,0:T(8,128)(2,1)}, bf16[512,512]{1,0:T(8,128)(2,1)}, /*index=5*/f32[1,128]{1,0:T(1,128)}) custom-call(bf16[2048,1024]{1,0:T(8,128)(2,1)} %features_home.1, f32[1,1024]{1,0:T(1,128)} %bitcast.6, s32[1,2048]{1,0:T(1,128)} %bitcast.5, ...), custom_call_target="tpu_custom_call" | custom-call | tf_op jit(solution)/shard_map/pallas_call | solution.py:607
  36.4 55.6 %shard_map.47 = (bf16[512,512]{1,0:T(8,128)(2,1)}, bf16[512,512]{1,0:T(8,128)(2,1)}) custom-call(f32[1,128]{1,0:T(1,128)} %get-tuple-element.14.size, f32[512,512]{1,0:T(8,128)} %get-tuple-element.15.gram_home, bf16[512,512]{1,0:T(8,128)(2,1)} %get-tuple-element.16._upper, ...), custom_call_target="tpu_custom_call", output_to_operand_aliasing={{0}: (2, {}), {1}: (3, {})} | custom-call | tf_op jit(solution)/shard_map/pallas_call | solution.py:648
  92.1 31.0 %shard_map.48 = f32[1,1024]{1,0:T(1,128)} custom-call(bf16[2048,512]{1,0:T(8,128)(2,1)} %get-tuple-element.13.scaled_home, bf16[512,512]{1,0:T(8,128)(2,1)} %get-tuple-element.18.upper, bf16[512,512]{1,0:T(8,128)(2,1)} %get-tuple-element.19.lower, f32[1,512]{1,0:T(1,128)} %get-tuple-element.20.gradient), custom_call_target="tpu_custom_call" | custom-call | tf_op jit(solution)/shard_map/pallas_call | solution.py:662
  123.0 1.3 %copy.10 = f32[1024]{0:T(1024)} copy(f32[1024]{0:T(1024)} %bitcast.4) | data formatting | bytes 8192

commit v6 on v5

--- a/solution.py
+++ b/solution.py
@@ -265,10 +265,9 @@
     load_other.start()
     load_mine.start()
     wait_all = greet([partner] + across + along)
-    names = jnp.transpose(jnp.broadcast_to(sampled[...], (128, samples)))
 
     def choose(first):
-        wanted = names[first : first + piece]
+        wanted = jnp.transpose(jnp.broadcast_to(sampled[:, first : first + piece], (128, piece)))
         lane = lax.broadcasted_iota(jnp.int32, wanted.shape, 1)
         for start in range(0, rows, 128):
             hot = jnp.where(lane + start == wanted, 1.0, 0.0)
@@ -441,12 +440,14 @@
     pair[order:] = top
     pair[:order] = (eye - mxu(unit_top, top, 1, 0)).astype(jnp.bfloat16)
     raise_power(inverse, pair, 2)
+    pair[:order] = unit_top
+    pair[order:] = unit_low
     left = None
     for _ in range(POLISH):
         value = inverse[...]
         top, low = halves(value)
-        product = mxu(unit_top, top, 1, 0) + mxu(unit_top, low, 1, 0) + mxu(unit_low, top, 1, 0)
-        left = eye - product
+        product = mxu(pair[...], top, 1, 0)
+        left = eye - (product[:order] + (product[order:] + mxu(pair[:order], low, 1, 0)))
         inverse[...] = value + mxu(top, left.astype(jnp.bfloat16), 1, 0)
     top, low = halves(inverse[...] / bound)
     upper[...] = top

time: 125 us -> 125 us (level); the launches traced: 124 us -> 126 us
  no operation moved by 1% of the time
where the time goes in v6:
time: 125 us; the launch traced here: 126 us
  Pallas kernels  124 us (99%)
  local copies, waits for them, and re-layouts  1.28 us (1%)
    pallas_call x1, Pallas kernels, split_device(): pl.pallas_call(rescue_kernel, out_shape=(shaped((half, half), jnp.bfloat1...  55.6 us
    pallas_call x1, Pallas kernels, split_device(): pl.pallas_call(functools.partial(gram_kernel, layers), out_shape=(shaped(...  36.6 us
    pallas_call x1, Pallas kernels, split_device(): pl.pallas_call(functools.partial(descent_kernel, layers), out_shape=shape...  32 us

profile of v6, /device:TPU:0, one launch (start us, length us, event | category | flops | bytes accessed | tf_op | source)
XLA Modules:
  0.0 125.6 jit_solution(5429382231475700665)
XLA Ops:
  0.0 36.6 %shard_map.46 = (bf16[2048,512]{1,0:T(8,128)(2,1)}, f32[512,512]{1,0:T(8,128)}, f32[1,512]{1,0:T(1,128)}, bf16[512,512]{1,0:T(8,128)(2,1)}, bf16[512,512]{1,0:T(8,128)(2,1)}, /*index=5*/f32[1,128]{1,0:T(1,128)}) custom-call(bf16[2048,1024]{1,0:T(8,128)(2,1)} %features_home.1, f32[1,1024]{1,0:T(1,128)} %bitcast.6, s32[1,2048]{1,0:T(1,128)} %bitcast.5, ...), custom_call_target="tpu_custom_call" | custom-call | tf_op jit(solution)/shard_map/pallas_call | solution.py:608
  36.6 55.6 %shard_map.47 = (bf16[512,512]{1,0:T(8,128)(2,1)}, bf16[512,512]{1,0:T(8,128)(2,1)}) custom-call(f32[1,128]{1,0:T(1,128)} %get-tuple-element.14.size, f32[512,512]{1,0:T(8,128)} %get-tuple-element.15.gram_home, bf16[512,512]{1,0:T(8,128)(2,1)} %get-tuple-element.16._upper, ...), custom_call_target="tpu_custom_call", output_to_operand_aliasing={{0}: (2, {}), {1}: (3, {})} | custom-call | tf_op jit(solution)/shard_map/pallas_call | solution.py:649
  92.3 32.0 %shard_map.48 = f32[1,1024]{1,0:T(1,128)} custom-call(bf16[2048,512]{1,0:T(8,128)(2,1)} %get-tuple-element.13.scaled_home, bf16[512,512]{1,0:T(8,128)(2,1)} %get-tuple-element.18.upper, bf16[512,512]{1,0:T(8,128)(2,1)} %get-tuple-element.19.lower, f32[1,512]{1,0:T(1,128)} %get-tuple-element.20.gradient), custom_call_target="tpu_custom_call" | custom-call | tf_op jit(solution)/shard_map/pallas_call | solution.py:663
  124.3 1.3 %copy.10 = f32[1024]{0:T(1024)} copy(f32[1024]{0:T(1024)} %bitcast.4) | data formatting | bytes 8192
